TPU v7x, 32 devices: a whole 2x2x4 slice. The times are simulated.
32 devices in a mesh: lat: 4 (over y, x), lon: 8 (over z, core).
Axes of the slice: x: 2, y: 2, z: 4, core: 2. Of those that a mesh axis runs over, the one named last changes fastest.
Arguments:
- patches: bfloat16 [128, 256, 1280], P('lat', 'lon'), may hold values from -6 to 6
- w_embed: bfloat16 [1280, 1024], replicated, may hold values from -0.15625 to 0.15625
- b_embed: float32 [1024], replicated, may hold values from -2 to 2
- pos_embed: bfloat16 [128, 256, 1024], P('lat', 'lon'), may hold values from -3 to 3
- gain_one: float32 [1024], replicated, may hold values from 0.1 to 1.9
- shift_one: float32 [1024], replicated, may hold values from -2 to 2
- w_spec_one: bfloat16 [2, 8, 128, 128], replicated, may hold values from -0.375 to 0.375
- b_spec_one: float32 [2, 8, 128], replicated, may hold values from -2 to 2
- w_spec_two: bfloat16 [2, 8, 128, 128], replicated, may hold values from -0.375 to 0.375
- b_spec_two: float32 [2, 8, 128], replicated, may hold values from -2 to 2
- gain_two: float32 [1024], replicated, may hold values from 0.1 to 1.9
- shift_two: float32 [1024], replicated, may hold values from -2 to 2
- w_fc_one: bfloat16 [1024, 4096], replicated, may hold values from -0.1875 to 0.1875
- b_fc_one: float32 [4096], replicated, may hold values from -2 to 2
- w_fc_two: bfloat16 [4096, 1024], replicated, may hold values from -0.09375 to 0.09375
- b_fc_two: float32 [1024], replicated, may hold values from -2 to 2
Outputs:
- block_out: bfloat16 [128, 256, 1024], P('lat', 'lon')
All inputs are finite; a program needn't handle non-finite values.
Results may differ from a plain program's by a relative error of at most 0.01.
Values may be sent and summed in bfloat16 or wider, within the bound.
A program may use at most 128 MiB of HBM per device.

v0:
```python
import math

import jax
import jax.numpy as jnp
from jax import lax
from jax.sharding import PartitionSpec as P


def angle_table(length, mode_count):
    product = (
        jnp.arange(mode_count, dtype=jnp.int32)[:, None]
        * jnp.arange(length, dtype=jnp.int32)[None, :]
        % length
    )
    phase = product.astype(jnp.float32) * (2.0 * math.pi / length)
    return (jnp.cos(phase), jnp.sin(phase))


def layer_norm(values, gain_vec, shift_vec):
    floats = values.astype(jnp.float32)
    center = jnp.mean(floats, axis=-1, keepdims=True)
    spread = jnp.mean(jnp.square(floats - center), axis=-1, keepdims=True)
    return (floats - center) * lax.rsqrt(spread + 1e-06) * gain_vec + shift_vec


def shrink(values):
    return jnp.where(
        values > 0.01,
        values - 0.01,
        jnp.where(values < -0.01, values + 0.01, jnp.zeros_like(values)),
    )


def contract(table, field, form):
    return jnp.einsum(form, table, field, preferred_element_type=jnp.float32)


def block_mix(real_part, imag_part, weights):
    form = "nbi,bio->nbo"
    out_re = contract(real_part, weights[0], form) - contract(imag_part, weights[1], form)
    out_im = contract(real_part, weights[1], form) + contract(imag_part, weights[0], form)
    return (out_re, out_im)


def per_device(
    patches,
    w_embed,
    b_embed,
    pos_embed,
    gain_one,
    shift_one,
    w_spec_one,
    b_spec_one,
    w_spec_two,
    b_spec_two,
    gain_two,
    shift_two,
    w_fc_one,
    b_fc_one,
    w_fc_two,
    b_fc_two,
):
    lat_count = lax.axis_size("lat")
    lon_count = lax.axis_size("lon")
    tile_rows, tile_cols, patch_len = patches.shape
    width = w_embed.shape[1]
    total_rows = tile_rows * lat_count
    total_cols = tile_cols * lon_count
    wave_count = total_cols // 2
    own_waves = wave_count // (lat_count * lon_count)
    block_count = w_spec_one.shape[1]
    block_size = w_spec_one.shape[2]
    scale = 1.0 / math.sqrt(total_rows * total_cols)
    tokens = tile_rows * tile_cols
    flat = jnp.dot(patches.reshape(tokens, patch_len), w_embed, preferred_element_type=jnp.float32)
    embedded = (flat + b_embed + pos_embed.reshape(tokens, width).astype(jnp.float32)).astype(
        jnp.bfloat16
    )
    normed = layer_norm(embedded, gain_one, shift_one).astype(jnp.bfloat16)
    circles = lax.all_to_all(
        normed.reshape(tile_rows, tile_cols, width), "lon", split_axis=0, concat_axis=1, tiled=True
    )
    cos_w, sin_w = angle_table(total_cols, wave_count)
    fwd_cos = cos_w.T.astype(jnp.bfloat16)
    fwd_sin = (-sin_w).T.astype(jnp.bfloat16)
    lon_re = contract(circles, fwd_cos, "rwd,wk->rkd").astype(jnp.bfloat16)
    lon_im = contract(circles, fwd_sin, "rwd,wk->rkd").astype(jnp.bfloat16)
    col_re, col_im = (
        lax.all_to_all(lon_re, ("lat", "lon"), split_axis=1, concat_axis=0, tiled=True),
        lax.all_to_all(lon_im, ("lat", "lon"), split_axis=1, concat_axis=0, tiled=True),
    )
    cos_h, sin_h = angle_table(total_rows, total_rows)
    cos_h = cos_h.astype(jnp.bfloat16)
    sin_h = sin_h.astype(jnp.bfloat16)
    form = "qh,hkd->qkd"
    spec_re = (scale * (contract(cos_h, col_re, form) + contract(sin_h, col_im, form))).astype(
        jnp.bfloat16
    )
    spec_im = (scale * (contract(cos_h, col_im, form) - contract(sin_h, col_re, form))).astype(
        jnp.bfloat16
    )
    mode_shape = (total_rows * own_waves, block_count, block_size)
    mix_re, mix_im = block_mix(spec_re.reshape(mode_shape), spec_im.reshape(mode_shape), w_spec_one)
    first_re = jax.nn.relu(mix_re + b_spec_one[0]).astype(jnp.bfloat16)
    first_im = jax.nn.relu(mix_im + b_spec_one[1]).astype(jnp.bfloat16)
    mix_re, mix_im = block_mix(first_re, first_im, w_spec_two)
    shrunk_re = (
        shrink(mix_re + b_spec_two[0]).astype(jnp.bfloat16).reshape(total_rows, own_waves, width)
    )
    shrunk_im = (
        shrink(mix_im + b_spec_two[1]).astype(jnp.bfloat16).reshape(total_rows, own_waves, width)
    )
    back_re = (contract(cos_h, shrunk_re, form) - contract(sin_h, shrunk_im, form)).astype(
        jnp.bfloat16
    )
    back_im = (contract(sin_h, shrunk_re, form) + contract(cos_h, shrunk_im, form)).astype(
        jnp.bfloat16
    )
    cycle_re, cycle_im = (
        lax.all_to_all(back_re, ("lat", "lon"), split_axis=0, concat_axis=1, tiled=True),
        lax.all_to_all(back_im, ("lat", "lon"), split_axis=0, concat_axis=1, tiled=True),
    )
    weight_k = jnp.where(jnp.arange(wave_count, dtype=jnp.int32) == 0, 1.0, 2.0).astype(
        jnp.float32
    )[:, None]
    inv_cos = (weight_k * cos_w).astype(jnp.bfloat16)
    inv_sin = (weight_k * sin_w).astype(jnp.bfloat16)
    filtered = (
        scale
        * (contract(cycle_re, inv_cos, "rkd,kw->rwd") - contract(cycle_im, inv_sin, "rkd,kw->rwd"))
    ).astype(jnp.bfloat16)
    filtered = lax.all_to_all(filtered, "lon", split_axis=1, concat_axis=0, tiled=True).reshape(
        tokens, width
    )
    mixed = (
        filtered.astype(jnp.float32) + normed.astype(jnp.float32) + embedded.astype(jnp.float32)
    ).astype(jnp.bfloat16)
    normed_two = layer_norm(mixed, gain_two, shift_two).astype(jnp.bfloat16)
    hidden = jax.nn.gelu(
        jnp.dot(normed_two, w_fc_one, preferred_element_type=jnp.float32) + b_fc_one,
        approximate=False,
    ).astype(jnp.bfloat16)
    result = (
        mixed.astype(jnp.float32)
        + jnp.dot(hidden, w_fc_two, preferred_element_type=jnp.float32)
        + b_fc_two
    )
    return result.astype(jnp.bfloat16).reshape(tile_rows, tile_cols, width)


def solution(mesh):
    in_specs = (
        P("lat", "lon", None),
        P(),
        P(),
        P("lat", "lon", None),
        P(),
        P(),
        P(),
        P(),
        P(),
        P(),
        P(),
        P(),
        P(),
        P(),
        P(),
        P(),
    )
    out_specs = P("lat", "lon", None)
    return jax.shard_map(
        per_device, mesh=mesh, in_specs=in_specs, out_specs=out_specs, check_vma=False
    )
```

profile of v0, /device:TPU:0, one launch (start us, length us, event | category | flops | bytes accessed | tf_op | source)
XLA Modules:
  0.0 340.3 jit_solution(14356329836799909401)
XLA Ops:
  0.0 1.7 copy-done
  1.7 5.4 %convert_reduce_fusion.1 = (f32[1024]{0:T(1024)S(1)}, bf16[1024,1024]{1,0:T(8,128)(2,1)S(1)}) fusion(bf16[32,32,1024]{2,1,0:T(8,128)(2,1)} %param.19, f32[1024]{0:T(1024)} %param.18, bf16[1024,1280]{1,0:T(8,128)(2,1)S(1)} %bitcast.126, bf16[1280,1024]{1,0:T(8,128)(2,1)} %param.17), kind=kOutput, calls=%fused_computation.26 | convolution fusion | flops 2690644992 | bytes 9445376 | tf_op jit(solution)/shard_map/dot_general | solution.py:75
  7.2 0.7 fusion.22
  7.9 0.8 fusion.25
  8.7 55.2 %all_to_all.99 = bf16[32,32,1024]{2,1,0:T(8,128)(2,1)S(1)} all-to-all(bf16[32,32,1024]{2,1,0:T(8,128)(2,1)S(1)} %bitcast.131), channel_id=1, replica_groups=mesh['lat'=4,'lon'=8] {'lon'}, dimensions={0} | all-to-all | bytes 4194304 | tf_op jit(solution)/shard_map/all_to_all | solution.py:80
  63.9 0.2 copy.41
  64.1 0.9 fusion.44
  65.0 1.8 copy.44
  66.8 3.5 %all-to-all-start.2 = ((bf16[4,128,1024]{2,0,1:T(4,128)(2,1)}), bf16[4,128,1024]{2,0,1:T(4,128)(2,1)S(1)}, u32[]{:S(2)}, u32[]{:S(2)}) async-start(bf16[4,128,1024]{2,0,1:T(4,128)(2,1)} %copy.44), calls=%async_computation.2 | async-start | bytes 2097152 | tf_op jit(solution)/shard_map/all_to_all | solution.py:90
  70.4 0.0 copy-start.11
  70.4 0.9 fusion.43
  71.3 1.8 copy.42
  73.1 24.7 %all-to-all-done.2 = bf16[4,128,1024]{2,0,1:T(4,128)(2,1)S(1)} async-done(((bf16[4,128,1024]{2,0,1:T(4,128)(2,1)}), bf16[4,128,1024]{2,0,1:T(4,128)(2,1)S(1)}, u32[]{:S(2)}, u32[]{:S(2)}) %all-to-all-start.2) | async-done | bytes 1048608 | tf_op jit(solution)/shard_map/all_to_all | solution.py:90
  97.8 2.8 all-to-all-start.1
  100.7 1.4 copy.86
  102.1 1.3 all_to_all.83
  103.4 24.7 %all-to-all-done.1 = bf16[4,128,1024]{2,0,1:T(4,128)(2,1)S(1)} async-done(((bf16[4,128,1024]{2,0,1:T(4,128)(2,1)}), bf16[4,128,1024]{2,0,1:T(4,128)(2,1)S(1)}, u32[]{:S(2)}, u32[]{:S(2)}) %all-to-all-start.1) | async-done | bytes 1048608 | tf_op jit(solution)/shard_map/all_to_all | solution.py:89
  128.1 0.4 copy.87
  128.5 0.3 all_to_all.79
  128.8 0.6 fusion.122
  129.4 2.0 fusion.120
  131.4 0.7 multiply_convert_fusion.2
  132.1 0.8 copy.46
  133.0 0.4 reshape.68
  133.4 2.8 fusion.57
  136.3 2.7 fusion.59
  138.9 0.7 multiply_convert_fusion.1
  139.6 1.8 copy.48
  141.4 1.5 reshape.69
  142.9 1.5 fusion.45
  144.4 0.4 fusion.61
  144.9 1.7 fusion.65
  146.6 0.5 fusion.46
  147.1 0.8 fusion.48
  147.9 0.7 copy.54
  148.6 0.3 reshape.71
  148.9 2.5 fusion.47
  151.4 0.7 copy.52
  152.1 0.5 reshape.70
  152.6 1.1 fusion.51
  153.7 1.1 add_convert_fusion
  154.8 1.8 copy.60
  156.6 2.6 all-to-all-start.4
  159.2 1.1 fusion.53
  160.3 1.1 subtract_convert_fusion
  161.4 1.8 copy.56
  163.2 23.5 %all-to-all-done.4 = bf16[128,4,1024]{2,1,0:T(4,128)(2,1)S(1)} async-done(((bf16[128,4,1024]{2,1,0:T(4,128)(2,1)}), bf16[128,4,1024]{2,1,0:T(4,128)(2,1)S(1)}, u32[]{:S(2)}, u32[]{:S(2)}) %all-to-all-start.4) | async-done | bytes 1048608 | tf_op jit(solution)/shard_map/all_to_all | solution.py:121
  186.7 2.6 all-to-all-start.3
  189.3 0.4 copy.84
  189.7 0.3 all_to_all.91
  190.0 26.8 %all-to-all-done.3 = bf16[128,4,1024]{2,1,0:T(4,128)(2,1)S(1)} async-done(((bf16[128,4,1024]{2,1,0:T(4,128)(2,1)}), bf16[128,4,1024]{2,1,0:T(4,128)(2,1)S(1)}, u32[]{:S(2)}, u32[]{:S(2)}) %all-to-all-start.3) | async-done | bytes 1048608 | tf_op jit(solution)/shard_map/all_to_all | solution.py:120
  216.8 0.4 copy.85
  217.2 0.3 all_to_all.87
  217.5 1.1 fusion.95
  218.6 1.2 fusion.42
  219.8 1.6 copy.62
  221.4 0.0 slice-start
  221.4 52.0 %all_to_all.100 = bf16[4,256,1024]{2,0,1:T(4,128)(2,1)S(1)} all-to-all(bf16[4,256,1024]{2,0,1:T(4,128)(2,1)S(1)} %copy.62), channel_id=1, replica_groups=mesh['lat'=4,'lon'=8] {'lon'}, dimensions={1} | all-to-all | bytes 4194304 | tf_op jit(solution)/shard_map/all_to_all | solution.py:132
  273.4 0.8 copy.63
  274.2 0.8 copy-done.3
  275.0 2.3 convert_reduce_fusion
  277.3 0.7 fusion.18
  278.1 49.2 %fusion.228 = bf16[1024,4096]{1,0:T(8,128)(2,1)} fusion(f32[4096]{0:T(1024)S(1)} %copy-done.14, bf16[1024,4096]{1,0:T(8,128)(2,1)S(1)} %bitcast.141, bf16[1024,1024]{1,0:T(8,128)(2,1)S(1)} %get-tuple-element.6, f32[1024]{0:T(1024)S(1)} %copy-done.15, f32[1024]{0:T(1024)S(1)} %copy-done.16, f32[1024]{0:T(1024)S(1)} %add_rsqrt_fusion, ...), kind=kOutput, calls=%fused_computation.3.clone.clone.clone.clone.1 | convolution fusion | flops 8873050112 | bytes 18907136 | tf_op jit(solution)/shard_map/dot_general | solution.py:140
  327.3 12.6 %fusion.28 = bf16[1024,1024]{1,0:T(8,128)(2,1)} fusion(bf16[1024,1024]{1,0:T(8,128)(2,1)S(1)} %get-tuple-element.6, bf16[4096,1024]{1,0:T(8,128)(2,1)S(1)} %copy-done.13, f32[1024]{0:T(1024)S(1)} %copy-done.17, bf16[1024,4096]{1,0:T(8,128)(2,1)} %fusion.228), kind=kOutput, calls=%fused_computation.41 | convolution fusion | flops 8594128896 | bytes 20975616 | tf_op jit(solution)/shard_map/dot_general | solution.py:145
  (44 shorter events, 0.1 us)
Async XLA Ops:
  0.0 1.7 copy-start
  1.7 6.2 %copy-start.9 = (f32[1024]{0:T(1024)S(1)}, f32[1024]{0:T(1024)}, u32[]{:S(2)}) copy-start(f32[1024]{0:T(1024)} %param.21) | copy-start | bytes 12292
  1.7 6.2 %copy-start.10 = (f32[1024]{0:T(1024)S(1)}, f32[1024]{0:T(1024)}, u32[]{:S(2)}) copy-start(f32[1024]{0:T(1024)} %param.20) | copy-start | bytes 12292
  7.2 56.8 %copy-start.2 = (bf16[1024,1024]{1,0:T(8,128)(2,1)}, bf16[1024,1024]{1,0:T(8,128)(2,1)S(1)}, u32[]{:S(2)}) copy-start(bf16[1024,1024]{1,0:T(8,128)(2,1)S(1)} %get-tuple-element.12) | copy-start | bytes 6291460
  66.8 31.0 %all-to-all-start.2 = ((bf16[4,128,1024]{2,0,1:T(4,128)(2,1)}), bf16[4,128,1024]{2,0,1:T(4,128)(2,1)S(1)}, u32[]{:S(2)}, u32[]{:S(2)}) async-start(bf16[4,128,1024]{2,0,1:T(4,128)(2,1)} %copy.44), calls=%async_computation.2 | async-start | bytes 2097152 | tf_op jit(solution)/shard_map/all_to_all | solution.py:90
  70.4 30.3 %copy-start.11 = (f32[2,8,128]{2,1,0:T(8,128)S(1)}, f32[2,8,128]{2,1,0:T(8,128)}, u32[]{:S(2)}) copy-start(f32[2,8,128]{2,1,0:T(8,128)} %param.23) | copy-start | bytes 24580
  70.4 30.3 %copy-start.12 = (f32[2,8,128]{2,1,0:T(8,128)S(1)}, f32[2,8,128]{2,1,0:T(8,128)}, u32[]{:S(2)}) copy-start(f32[2,8,128]{2,1,0:T(8,128)} %param.25) | copy-start | bytes 24580
  97.8 30.3 %all-to-all-start.1 = ((bf16[4,128,1024]{2,0,1:T(4,128)(2,1)}), bf16[4,128,1024]{2,0,1:T(4,128)(2,1)S(1)}, u32[]{:S(2)}, u32[]{:S(2)}) async-start(bf16[4,128,1024]{2,0,1:T(4,128)(2,1)} %copy.42), calls=%async_computation.1 | async-start | bytes 2097152 | tf_op jit(solution)/shard_map/all_to_all | solution.py:89
  133.4 5.5 %copy-start.5 = (f32[128,4,1024]{2,0,1:T(8,128)S(1)}, f32[128,4,1024]{2,0,1:T(8,128)}, u32[]{:S(2)}) copy-start(f32[128,4,1024]{2,0,1:T(8,128)} %fusion.120) | copy-start | bytes 6291460
  138.9 4.0 %copy-start.6 = (f32[8,512,128]{2,1,0:T(8,128)S(1)}, f32[8,512,128]{2,1,0:T(8,128)}, u32[]{:S(2)}) copy-start(f32[8,512,128]{2,1,0:T(8,128)} %fusion.59) | copy-start | bytes 6291460
  142.9 1.5 copy-start.8
  144.4 2.2 copy-start.4
  144.4 2.2 copy-start.7
  156.6 30.1 %all-to-all-start.4 = ((bf16[128,4,1024]{2,1,0:T(4,128)(2,1)}), bf16[128,4,1024]{2,1,0:T(4,128)(2,1)S(1)}, u32[]{:S(2)}, u32[]{:S(2)}) async-start(bf16[128,4,1024]{2,1,0:T(4,128)(2,1)} %copy.60), calls=%async_computation.4 | async-start | bytes 2097152 | tf_op jit(solution)/shard_map/all_to_all | solution.py:121
  186.7 30.1 %all-to-all-start.3 = ((bf16[128,4,1024]{2,1,0:T(4,128)(2,1)}), bf16[128,4,1024]{2,1,0:T(4,128)(2,1)S(1)}, u32[]{:S(2)}, u32[]{:S(2)}) async-start(bf16[128,4,1024]{2,1,0:T(4,128)(2,1)} %copy.56), calls=%async_computation.3 | async-start | bytes 2097152 | tf_op jit(solution)/shard_map/all_to_all | solution.py:120
  221.4 56.6 %slice-start = ((s8[8388608]{0:T(1024)(128)(4,1)}), s8[4194304]{0:T(1024)(128)(4,1)S(1)}, s32[]{:S(2)}) async-start(s8[8388608]{0:T(1024)(128)(4,1)} %bitcast.140), calls=%async_computation.6 | async-start | bytes 8388608
  273.4 1.6 copy-start.3
  275.0 3.0 slice-start.1
  275.0 3.0 copy-start.14
  275.0 3.0 copy-start.15
  275.0 3.0 copy-start.16
  278.1 49.2 %copy-start.13 = (bf16[4096,1024]{1,0:T(8,128)(2,1)S(1)}, bf16[4096,1024]{1,0:T(8,128)(2,1)}, u32[]{:S(2)}) copy-start(bf16[4096,1024]{1,0:T(8,128)(2,1)} %param.30) | copy-start | bytes 25165828
  278.1 49.2 %copy-start.17 = (f32[1024]{0:T(1024)S(1)}, f32[1024]{0:T(1024)}, u32[]{:S(2)}) copy-start(f32[1024]{0:T(1024)} %param.31) | copy-start | bytes 12292
  327.3 12.6 %copy-start.1 = (bf16[32,32,1280]{2,1,0:T(8,128)(2,1)S(1)}, bf16[32,32,1280]{2,1,0:T(8,128)(2,1)}, u32[]{:S(2)}) copy-start(bf16[32,32,1280]{2,1,0:T(8,128)(2,1)} %param.16) | copy-start | bytes 7864324
where the time goes:
time: 346 us; the launch traced here: 340 us
  blocking collectives  107 us (31%)
  waiting for transfers between devices  99.6 us (29%)
  matrix products  92.6 us (27%)
  local copies, waits for them, and re-layouts  23.8 us (7%)
  starting transfers between devices  11.6 us (3%)
  other arithmetic  4.5 us (1%)
    all_to_all x1, blocking collectives, per_device(): lax.all_to_all(normed.reshape(tile_rows, tile_cols, width), 'lon', split_...  55.2 us
    all_to_all x1, blocking collectives, per_device(): lax.all_to_all(filtered, 'lon', split_axis=1, concat_axis=0, tiled=True)  52 us
    dot_general x1, matrix products, per_device(): jnp.dot(normed_two, w_fc_one, preferred_element_type=jnp.float32) + b_fc_one  49.2 us
    all_to_all x1, waiting for transfers between devices, per_device(): lax.all_to_all(back_re, ('lat', 'lon'), split_axis=0, concat_axis=1, tile...  26.8 us
    dot_general x20, matrix products, contract(): return jnp.einsum(form, table, field, preferred_element_type=jnp.float32)  25.4 us
    all_to_all x1, waiting for transfers between devices, per_device(): lax.all_to_all(lon_im, ('lat', 'lon'), split_axis=1, concat_axis=0, tiled...  24.7 us
    all_to_all x1, waiting for transfers between devices, per_device(): lax.all_to_all(lon_re, ('lat', 'lon'), split_axis=1, concat_axis=0, tiled...  24.7 us
    all_to_all x1, waiting for transfers between devices, per_device(): lax.all_to_all(back_im, ('lat', 'lon'), split_axis=0, concat_axis=1, tile...  23.5 us
  transfers between devices with their start and end apart: 4, of which 4 were waited for; matrix products, arithmetic and copies ran while one was open for 2% of the time, Pallas kernels for 0%

commit v1 on v0

--- a/solution.py
+++ b/solution.py
@@ -1,9 +1,18 @@
+import functools
 import math
 
 import jax
 import jax.numpy as jnp
+import numpy as np
 from jax import lax
+from jax.experimental import pallas as pl
+from jax.experimental.pallas import tpu as pltpu
 from jax.sharding import PartitionSpec as P
+
+MESH = pl.DeviceIdType.MESH
+FORWARD_CHUNKS = 8
+BACK_CHUNKS = 4
+AHEAD = 3
 
 
 def angle_table(length, mode_count):
@@ -40,6 +49,486 @@
     out_re = contract(real_part, weights[0], form) - contract(imag_part, weights[1], form)
     out_im = contract(real_part, weights[1], form) + contract(imag_part, weights[0], form)
     return (out_re, out_im)
+
+
+def host_tables(length, mode_count):
+    product = np.arange(mode_count)[:, None] * np.arange(length)[None, :] % length
+    phase = product.astype(np.float32) * np.float32(2.0 * math.pi / length)
+    return (np.cos(phase).astype(np.float32), np.sin(phase).astype(np.float32))
+
+
+def norm_rows(values, gain_row, shift_row):
+    floats = values.astype(jnp.float32)
+    center = jnp.mean(floats, axis=-1, keepdims=True)
+    floats = floats - center
+    spread = jnp.mean(floats * floats, axis=-1, keepdims=True)
+    return floats * lax.rsqrt(spread + 1e-06) * gain_row + shift_row
+
+
+def dot(left, right):
+    return jnp.dot(left, right, preferred_element_type=jnp.float32)
+
+
+def fused_kernel(
+    lat_count,
+    lon_count,
+    patches,
+    w_embed,
+    b_embed,
+    pos_embed,
+    gain_one,
+    shift_one,
+    w_spec_one,
+    b_spec_one,
+    w_spec_two,
+    b_spec_two,
+    gain_two,
+    shift_two,
+    w_fc_one,
+    b_fc_one,
+    w_fc_two,
+    b_fc_two,
+    lon_table,
+    lon_back,
+    lat_table,
+    lat_back,
+    out,
+    patches_v,
+    w_embed_v,
+    pos_v,
+    w_fc_one_v,
+    w_fc_two_v,
+    embedded,
+    normed,
+    circles,
+    waves,
+    columns,
+    modes,
+    back,
+    cycles,
+    filtered,
+    tokens_in,
+    total,
+    result,
+    in_sem,
+    out_sem,
+    s1,
+    r1,
+    s2,
+    r2,
+    s3,
+    r3,
+    s4,
+    r4,
+):
+    tile_rows, tile_cols, patch_len = patches_v.shape
+    width = w_embed_v.shape[1]
+    chans = circles.shape[3]
+    total_rows = tile_rows * lat_count
+    total_cols = tile_cols * lon_count
+    pair = columns.shape[2]
+    own_waves = pair // 2
+    pitch = modes.shape[0] // total_rows
+    scale = 1.0 / math.sqrt(total_rows * total_cols)
+    my_lat = lax.axis_index("lat")
+    my_lon = lax.axis_index("lon")
+    half = lon_count // 2
+    lon_steps = sorted(range(1, lon_count), key=lambda d: abs(d - half))
+    lat_steps = list(range(1, lat_count))
+
+    def lon_peer(step):
+        return lax.rem(my_lon + step, lon_count)
+
+    def lat_peer(step):
+        return lax.rem(my_lat + step, lat_count)
+
+    def fetch(source, target, index):
+        return pltpu.make_async_copy(source, target, in_sem.at[index])
+
+    first_copies = [
+        fetch(w_embed, w_embed_v, 0),
+        fetch(patches, patches_v, 1),
+        fetch(pos_embed, pos_v, 2),
+    ]
+    later_copies = [fetch(w_fc_one, w_fc_one_v, 3), fetch(w_fc_two, w_fc_two_v, 4)]
+    for copy in first_copies:
+        copy.start()
+
+    barrier = pltpu.get_barrier_semaphore()
+    for step in lon_steps:
+        pl.semaphore_signal(
+            barrier, inc=1, device_id={"lon": lon_peer(step)}, device_id_type=MESH
+        )
+    for step in lat_steps:
+        pl.semaphore_signal(
+            barrier, inc=1, device_id={"lat": lat_peer(step)}, device_id_type=MESH
+        )
+    pl.semaphore_wait(barrier, lon_count + lat_count - 2)
+
+    def exchange(axis, send, recv, send_sem, recv_sem, chunk, rows, peer, mine):
+        return pltpu.make_async_remote_copy(
+            src_ref=send.at[peer, rows],
+            dst_ref=recv.at[mine, rows],
+            send_sem=send_sem.at[chunk, peer],
+            recv_sem=recv_sem.at[chunk, mine],
+            device_id={axis: peer},
+            device_id_type=MESH,
+        )
+
+    def lon_send(send, recv, send_sem, recv_sem, chunk, rows):
+        for step in lon_steps:
+            exchange(
+                "lon", send, recv, send_sem, recv_sem, chunk, rows, lon_peer(step), my_lon
+            ).start()
+
+    def lat_send(send, recv, send_sem, recv_sem, chunk, rows):
+        for step in lat_steps:
+            exchange(
+                "lat", send, recv, send_sem, recv_sem, chunk, rows, lat_peer(step), my_lat
+            ).start()
+
+    def lon_arrive(send, recv, send_sem, recv_sem, chunk, rows):
+        for step in lon_steps:
+            peer = lon_peer(step)
+            exchange("lon", send, recv, send_sem, recv_sem, chunk, rows, peer, peer).wait_recv()
+
+    def lat_arrive(send, recv, send_sem, recv_sem, chunk, rows):
+        for step in lat_steps:
+            peer = lat_peer(step)
+            exchange("lat", send, recv, send_sem, recv_sem, chunk, rows, peer, peer).wait_recv()
+
+    def sent(axis, steps, peer_of, mine, send, recv, send_sem, recv_sem, chunk, rows):
+        for step in steps:
+            exchange(
+                axis, send, recv, send_sem, recv_sem, chunk, rows, peer_of(step), mine
+            ).wait_send()
+
+    front = (normed, circles, s1, r1)
+    over = (waves, columns, s2, r2)
+    under = (back, cycles, s3, r3)
+    home = (filtered, tokens_in, s4, r4)
+    fwd_rows = tile_rows // FORWARD_CHUNKS
+    back_rows = tile_rows // BACK_CHUNKS
+
+    for copy in first_copies:
+        copy.wait()
+    for copy in later_copies:
+        copy.start()
+
+    @pl.loop(0, FORWARD_CHUNKS)
+    def embed_step(chunk):
+        rows = pl.ds(chunk * fwd_rows, fwd_rows)
+        count = fwd_rows * tile_cols
+        flat = dot(patches_v[rows].reshape(count, patch_len), w_embed_v[...])
+        flat = flat + b_embed[...] + pos_v[rows].reshape(count, width).astype(jnp.float32)
+        rounded = flat.astype(jnp.bfloat16)
+        embedded[rows] = rounded.reshape(fwd_rows, tile_cols, width)
+        scaled = norm_rows(rounded, gain_one[...], shift_one[...]).astype(jnp.bfloat16)
+        for block in range(lon_count):
+            piece = scaled[:, block * chans : (block + 1) * chans]
+            normed[block, rows] = piece.reshape(fwd_rows, tile_cols, chans)
+        lon_send(*front, chunk, rows)
+        circles[my_lon, rows] = normed[my_lon, rows]
+
+    @pl.loop(0, FORWARD_CHUNKS)
+    def wave_step(chunk):
+        rows = pl.ds(chunk * fwd_rows, fwd_rows)
+        lon_arrive(*front, chunk, rows)
+        for row in range(0, fwd_rows, 2):
+            base = chunk * fwd_rows + row
+            field = jnp.concatenate(
+                [circles[:, base + i].reshape(total_cols, chans) for i in range(2)], axis=1
+            )
+            spectrum = dot(lon_table[...], field).astype(jnp.bfloat16)
+            for owner in range(lat_count):
+                for i in range(2):
+                    waves[owner, base + i] = spectrum[
+                        owner * pair : (owner + 1) * pair, i * chans : (i + 1) * chans
+                    ]
+        lat_send(*over, chunk, rows)
+        columns[my_lat, rows] = waves[my_lat, rows]
+
+    @pl.loop(0, FORWARD_CHUNKS)
+    def widen_step(chunk):
+        rows = pl.ds(chunk * fwd_rows, fwd_rows)
+        lat_arrive(*over, chunk, rows)
+        for owner in range(lat_count):
+            for row in range(fwd_rows):
+                place = (owner * tile_rows + chunk * fwd_rows + row) * pitch
+                modes[pl.ds(pl.multiple_of(place, 8), pair), :] = columns[
+                    owner, chunk * fwd_rows + row
+                ].astype(jnp.float32)
+
+    def mix_matrix(weights):
+        real, imag = weights[0, my_lon], weights[1, my_lon]
+        return jnp.concatenate(
+            [
+                jnp.concatenate([real, imag], axis=1),
+                jnp.concatenate([-imag, real], axis=1),
+            ],
+            axis=0,
+        )
+
+    def mix_bias(bias):
+        return jnp.concatenate(
+            [bias[0, pl.ds(my_lon, 1), :], bias[1, pl.ds(my_lon, 1), :]], axis=1
+        )
+
+    mix_one, mix_two = mix_matrix(w_spec_one), mix_matrix(w_spec_two)
+    bias_one, bias_two = mix_bias(b_spec_one), mix_bias(b_spec_two)
+    group = 8
+
+    @pl.loop(0, own_waves // group)
+    def mode_step(step):
+        def place(i, part):
+            return pl.ds(step * group + i + part * own_waves, total_rows, stride=pitch)
+
+        field = jnp.concatenate(
+            [
+                jnp.concatenate([modes[place(i, 0), :], modes[place(i, 1), :]], axis=0).astype(
+                    jnp.bfloat16
+                )
+                for i in range(group)
+            ],
+            axis=1,
+        )
+        spec = (scale * dot(lat_table[...], field)).astype(jnp.bfloat16)
+        stacked = jnp.concatenate(
+            [
+                jnp.concatenate(
+                    [
+                        spec[:total_rows, i * chans : (i + 1) * chans],
+                        spec[total_rows:, i * chans : (i + 1) * chans],
+                    ],
+                    axis=1,
+                )
+                for i in range(group)
+            ],
+            axis=0,
+        )
+        first = jnp.maximum(dot(stacked, mix_one) + bias_one, 0.0).astype(jnp.bfloat16)
+        second = shrink(dot(first, mix_two) + bias_two).astype(jnp.bfloat16)
+        turned = jnp.concatenate(
+            [
+                jnp.concatenate(
+                    [
+                        second[i * total_rows : (i + 1) * total_rows, :chans],
+                        second[i * total_rows : (i + 1) * total_rows, chans:],
+                    ],
+                    axis=0,
+                )
+                for i in range(group)
+            ],
+            axis=1,
+        )
+        returned = dot(lat_back[...], turned)
+        for i in range(group):
+            modes[place(i, 0), :] = returned[:total_rows, i * chans : (i + 1) * chans]
+            modes[place(i, 1), :] = returned[total_rows:, i * chans : (i + 1) * chans]
+
+    @pl.loop(0, BACK_CHUNKS)
+    def return_step(chunk):
+        rows = pl.ds(chunk * back_rows, back_rows)
+        for owner in range(lat_count):
+            for row in range(back_rows):
+                place = (owner * tile_rows + chunk * back_rows + row) * pitch
+                back[owner, chunk * back_rows + row] = modes[
+                    pl.ds(pl.multiple_of(place, 8), pair), :
+                ].astype(jnp.bfloat16)
+        lat_send(*under, chunk, rows)
+        cycles[my_lat, rows] = back[my_lat, rows]
+
+    def inverse_step(chunk):
+        rows = pl.ds(chunk * back_rows, back_rows)
+        lat_arrive(*under, chunk, rows)
+        for row in range(0, back_rows, 2):
+            base = chunk * back_rows + row
+            field = jnp.concatenate(
+                [cycles[:, base + i].reshape(lat_count * pair, chans) for i in range(2)], axis=1
+            )
+            values = (scale * dot(lon_back[...], field)).astype(jnp.bfloat16)
+            for owner in range(lon_count):
+                for i in range(2):
+                    filtered[owner, base + i] = values[
+                        owner * tile_cols : (owner + 1) * tile_cols, i * chans : (i + 1) * chans
+                    ]
+        lon_send(*home, chunk, rows)
+        tokens_in[my_lon, rows] = filtered[my_lon, rows]
+
+    @pl.loop(0, AHEAD)
+    def inverse_ahead(chunk):
+        inverse_step(chunk)
+
+    for copy in later_copies:
+        copy.wait()
+    hidden_tile = b_fc_one.shape[1]
+
+    def out_copy(chunk):
+        rows = pl.ds(chunk * back_rows, back_rows)
+        return pltpu.make_async_copy(result.at[rows], out.at[rows], out_sem.at[chunk])
+
+    @pl.loop(0, BACK_CHUNKS)
+    def token_step(chunk):
+        rows = pl.ds(chunk * back_rows, back_rows)
+        count = back_rows * tile_cols
+        lon_arrive(*home, chunk, rows)
+
+        def gather(ref):
+            return jnp.concatenate(
+                [ref[block, rows].reshape(count, chans) for block in range(lon_count)], axis=1
+            ).astype(jnp.float32)
+
+        mixed = (
+            gather(tokens_in)
+            + gather(normed)
+            + embedded[rows].reshape(count, width).astype(jnp.float32)
+        ).astype(jnp.bfloat16)
+        lines = norm_rows(mixed, gain_two[...], shift_two[...]).astype(jnp.bfloat16)
+        total[...] = mixed.astype(jnp.float32) + b_fc_two[...]
+
+        @pl.loop(0, b_fc_one.shape[0])
+        def hidden_step(tile):
+            part = pl.ds(pl.multiple_of(tile * hidden_tile, hidden_tile), hidden_tile)
+            raw = dot(lines, w_fc_one_v[:, part]) + b_fc_one[pl.ds(tile, 1), :]
+            hidden = (0.5 * raw * (1.0 + lax.erf(raw * math.sqrt(0.5)))).astype(jnp.bfloat16)
+            total[...] += dot(hidden, w_fc_two_v[part, :])
+
+        result[rows] = total[...].astype(jnp.bfloat16).reshape(back_rows, tile_cols, width)
+        out_copy(chunk).start()
+
+        @pl.when(chunk + AHEAD < BACK_CHUNKS)
+        def inverse_rest():
+            inverse_step(chunk + AHEAD)
+
+    @pl.loop(0, FORWARD_CHUNKS)
+    def front_drain(chunk):
+        rows = pl.ds(chunk * fwd_rows, fwd_rows)
+        sent("lon", lon_steps, lon_peer, my_lon, *front, chunk, rows)
+        sent("lat", lat_steps, lat_peer, my_lat, *over, chunk, rows)
+
+    @pl.loop(0, BACK_CHUNKS)
+    def back_drain(chunk):
+        rows = pl.ds(chunk * back_rows, back_rows)
+        sent("lat", lat_steps, lat_peer, my_lat, *under, chunk, rows)
+        sent("lon", lon_steps, lon_peer, my_lon, *home, chunk, rows)
+        out_copy(chunk).wait()
+
+
+def per_device_fused(
+    patches,
+    w_embed,
+    b_embed,
+    pos_embed,
+    gain_one,
+    shift_one,
+    w_spec_one,
+    b_spec_one,
+    w_spec_two,
+    b_spec_two,
+    gain_two,
+    shift_two,
+    w_fc_one,
+    b_fc_one,
+    w_fc_two,
+    b_fc_two,
+):
+    lat_count = lax.axis_size("lat")
+    lon_count = lax.axis_size("lon")
+    tile_rows, tile_cols, patch_len = patches.shape
+    width = w_embed.shape[1]
+    hid = w_fc_one.shape[1]
+    total_rows = tile_rows * lat_count
+    total_cols = tile_cols * lon_count
+    wave_count = total_cols // 2
+    own_waves = wave_count // lat_count
+    pair = 2 * own_waves
+    pitch = pair + 8
+    chans = width // lon_count
+    cos_w, sin_w = host_tables(total_cols, wave_count)
+    cos_h, sin_h = host_tables(total_rows, total_rows)
+
+    def by_owner(real, imag):
+        shape = (lat_count, own_waves, total_cols)
+        both = np.stack([real.reshape(shape), imag.reshape(shape)], axis=1)
+        return both.reshape(2 * wave_count, total_cols)
+
+    weight_k = np.where(np.arange(wave_count) == 0, 1.0, 2.0).astype(np.float32)[:, None]
+    tables = [
+        by_owner(cos_w, -sin_w),
+        by_owner(weight_k * cos_w, -weight_k * sin_w).T,
+        np.block([[cos_h, sin_h], [-sin_h, cos_h]]),
+        np.block([[cos_h, -sin_h], [sin_h, cos_h]]),
+    ]
+    tables = [jnp.asarray(t, jnp.bfloat16) for t in tables]
+    hidden_tile = 512
+    vmem = pl.BlockSpec(memory_space=pltpu.VMEM)
+    hbm = pl.BlockSpec(memory_space=pl.ANY)
+    tile = (tile_rows, tile_cols, width)
+    by_lon = (lon_count, tile_rows, tile_cols, chans)
+    by_lat = (lat_count, tile_rows, pair, chans)
+    bf16 = jnp.bfloat16
+    dma = pltpu.SemaphoreType.DMA
+    return pl.pallas_call(
+        functools.partial(fused_kernel, lat_count, lon_count),
+        out_shape=jax.ShapeDtypeStruct(tile, bf16),
+        in_specs=[hbm, hbm, vmem, hbm, vmem, vmem, vmem, vmem, vmem, vmem, vmem, vmem]
+        + [hbm, vmem, hbm, vmem, vmem, vmem, vmem, vmem],
+        out_specs=hbm,
+        scratch_shapes=[
+            pltpu.VMEM(patches.shape, bf16),
+            pltpu.VMEM(w_embed.shape, bf16),
+            pltpu.VMEM(tile, bf16),
+            pltpu.VMEM(w_fc_one.shape, bf16),
+            pltpu.VMEM(w_fc_two.shape, bf16),
+            pltpu.VMEM(tile, bf16),
+            pltpu.VMEM(by_lon, bf16),
+            pltpu.VMEM(by_lon, bf16),
+            pltpu.VMEM(by_lat, bf16),
+            pltpu.VMEM(by_lat, bf16),
+            pltpu.VMEM((total_rows * pitch, chans), jnp.float32),
+            pltpu.VMEM(by_lat, bf16),
+            pltpu.VMEM(by_lat, bf16),
+            pltpu.VMEM(by_lon, bf16),
+            pltpu.VMEM(by_lon, bf16),
+            pltpu.VMEM((tile_rows // BACK_CHUNKS * tile_cols, width), jnp.float32),
+            pltpu.VMEM(tile, bf16),
+            dma((5,)),
+            dma((BACK_CHUNKS,)),
+            dma((FORWARD_CHUNKS, lon_count)),
+            dma((FORWARD_CHUNKS, lon_count)),
+            dma((FORWARD_CHUNKS, lat_count)),
+            dma((FORWARD_CHUNKS, lat_count)),
+            dma((BACK_CHUNKS, lat_count)),
+            dma((BACK_CHUNKS, lat_count)),
+            dma((BACK_CHUNKS, lon_count)),
+            dma((BACK_CHUNKS, lon_count)),
+        ],
+        compiler_params=pltpu.CompilerParams(
+            collective_id=0, has_side_effects=True, vmem_limit_bytes=66_000_000
+        ),
+    )(
+        patches,
+        w_embed,
+        b_embed.reshape(1, width),
+        pos_embed,
+        gain_one.reshape(1, width),
+        shift_one.reshape(1, width),
+        w_spec_one,
+        b_spec_one,
+        w_spec_two,
+        b_spec_two,
+        gain_two.reshape(1, width),
+        shift_two.reshape(1, width),
+        w_fc_one,
+        b_fc_one.reshape(hid // hidden_tile, hidden_tile),
+        w_fc_two,
+        b_fc_two.reshape(1, width),
+        *tables,
+    )
+
+
+def fits_fused(mesh):
+    return mesh.shape["lon"] == 8 and mesh.shape["lat"] <= 4
 
 
 def per_device(
@@ -168,6 +657,7 @@
         P(),
     )
     out_specs = P("lat", "lon", None)
+    body = per_device_fused if fits_fused(mesh) else per_device
     return jax.shard_map(
-        per_device, mesh=mesh, in_specs=in_specs, out_specs=out_specs, check_vma=False
-    )
+        body, mesh=mesh, in_specs=in_specs, out_specs=out_specs, check_vma=False
+    )

time: 346 us -> 136 us (0.39)
  the two profiles are of different devices: /device:TPU:0 before, /device:TPU:9 now
where the time goes in v1:
time: 136 us
  Pallas kernels  132 us (97%)
  local copies, waits for them, and re-layouts  4.51 us (3%)
    pallas_call x1, Pallas kernels, per_device_fused(): pl.pallas_call(functools.partial(fused_kernel, lat_count, lon_count), out...  132 us
    unnamed x1, local copies, waits for them, and re-layouts  3.19 us

profile of v1, /device:TPU:9, one launch (start us, length us, event | category | flops | bytes accessed | tf_op | source)
XLA Modules:
  0.0 136.1 jit_solution(8107484516958359367)
XLA Ops:
  0.0 1.3 reshape.26.b_fc_one
  1.3 131.6 %shard_map.190 = bf16[32,32,1024]{2,1,0:T(8,128)(2,1)} custom-call(bf16[32,32,1280]{2,1,0:T(8,128)(2,1)} %patches.1, bf16[1280,1024]{1,0:T(8,128)(2,1)} %w_embed.1, f32[1,1024]{1,0:T(1,128)} %bitcast.6, bf16[32,32,1024]{2,1,0:T(8,128)(2,1)} %pos_embed.1, f32[1,1024]{1,0:T(1,128)} %bitcast.7, f32[1,1024]{1,0:T(1,128)} %bitcast.8, ...), custom_call_target="tpu_custom_call" | custom-call | tf_op jit(solution)/shard_map/pallas_call | solution.py:471
  132.9 3.2 %copy.22 = bf16[32,32,1024]{2,1,0:T(8,128)(2,1)} copy(bf16[32,32,1024]{2,1,0:T(8,128)(2,1)} %shard_map.190) | data formatting | bytes 4194304

commit v2 on v1

--- a/solution.py
+++ b/solution.py
@@ -145,13 +145,19 @@
     def fetch(source, target, index):
         return pltpu.make_async_copy(source, target, in_sem.at[index])
 
+    lead = pl.ds(0, tile_rows // FORWARD_CHUNKS)
+    rest = pl.ds(tile_rows // FORWARD_CHUNKS, tile_rows - tile_rows // FORWARD_CHUNKS)
     first_copies = [
         fetch(w_embed, w_embed_v, 0),
-        fetch(patches, patches_v, 1),
-        fetch(pos_embed, pos_v, 2),
+        fetch(patches.at[lead], patches_v.at[lead], 1),
+        fetch(pos_embed.at[lead], pos_v.at[lead], 2),
+    ]
+    second_copies = [
+        fetch(patches.at[rest], patches_v.at[rest], 5),
+        fetch(pos_embed.at[rest], pos_v.at[rest], 6),
     ]
     later_copies = [fetch(w_fc_one, w_fc_one_v, 3), fetch(w_fc_two, w_fc_two_v, 4)]
-    for copy in first_copies:
+    for copy in first_copies + second_copies:
         copy.start()
 
     barrier = pltpu.get_barrier_semaphore()
@@ -212,10 +218,7 @@
 
     for copy in first_copies:
         copy.wait()
-    for copy in later_copies:
-        copy.start()
-
-    @pl.loop(0, FORWARD_CHUNKS)
+
     def embed_step(chunk):
         rows = pl.ds(chunk * fwd_rows, fwd_rows)
         count = fwd_rows * tile_cols
@@ -229,6 +232,26 @@
             normed[block, rows] = piece.reshape(fwd_rows, tile_cols, chans)
         lon_send(*front, chunk, rows)
         circles[my_lon, rows] = normed[my_lon, rows]
+
+    embed_step(0)
+    for copy in second_copies:
+        copy.wait()
+    for copy in later_copies:
+        copy.start()
+
+    @pl.loop(1, FORWARD_CHUNKS)
+    def embed_rest(chunk):
+        embed_step(chunk)
+
+    def widen_step(chunk):
+        rows = pl.ds(chunk * fwd_rows, fwd_rows)
+        lat_arrive(*over, chunk, rows)
+        for owner in range(lat_count):
+            for row in range(fwd_rows):
+                place = (owner * tile_rows + chunk * fwd_rows + row) * pitch
+                modes[pl.ds(pl.multiple_of(place, 8), pair), :] = columns[
+                    owner, chunk * fwd_rows + row
+                ].astype(jnp.float32)
 
     @pl.loop(0, FORWARD_CHUNKS)
     def wave_step(chunk):
@@ -248,16 +271,11 @@
         lat_send(*over, chunk, rows)
         columns[my_lat, rows] = waves[my_lat, rows]
 
-    @pl.loop(0, FORWARD_CHUNKS)
-    def widen_step(chunk):
-        rows = pl.ds(chunk * fwd_rows, fwd_rows)
-        lat_arrive(*over, chunk, rows)
-        for owner in range(lat_count):
-            for row in range(fwd_rows):
-                place = (owner * tile_rows + chunk * fwd_rows + row) * pitch
-                modes[pl.ds(pl.multiple_of(place, 8), pair), :] = columns[
-                    owner, chunk * fwd_rows + row
-                ].astype(jnp.float32)
+        @pl.when(chunk > 0)
+        def widen_previous():
+            widen_step(chunk - 1)
+
+    widen_step(FORWARD_CHUNKS - 1)
 
     def mix_matrix(weights):
         real, imag = weights[0, my_lon], weights[1, my_lon]
@@ -492,7 +510,7 @@
             pltpu.VMEM(by_lon, bf16),
             pltpu.VMEM((tile_rows // BACK_CHUNKS * tile_cols, width), jnp.float32),
             pltpu.VMEM(tile, bf16),
-            dma((5,)),
+            dma((7,)),
             dma((BACK_CHUNKS,)),
             dma((FORWARD_CHUNKS, lon_count)),
             dma((FORWARD_CHUNKS, lon_count)),

time: 136 us -> 136 us (level)
  no operation moved by 1% of the time
where the time goes in v2:
time: 136 us
  Pallas kernels  131 us (96%)
  local copies, waits for them, and re-layouts  4.51 us (3%)
    pallas_call x1, Pallas kernels, per_device_fused(): pl.pallas_call(functools.partial(fused_kernel, lat_count, lon_count), out...  131 us
    unnamed x1, local copies, waits for them, and re-layouts  3.19 us

profile of v2, /device:TPU:9, one launch (start us, length us, event | category | flops | bytes accessed | tf_op | source)
XLA Modules:
  0.0 135.6 jit_solution(9978011845426873996)
XLA Ops:
  0.0 1.3 reshape.26.b_fc_one
  1.3 131.0 %shard_map.190 = bf16[32,32,1024]{2,1,0:T(8,128)(2,1)} custom-call(bf16[32,32,1280]{2,1,0:T(8,128)(2,1)} %patches.1, bf16[1280,1024]{1,0:T(8,128)(2,1)} %w_embed.1, f32[1,1024]{1,0:T(1,128)} %bitcast.6, bf16[32,32,1024]{2,1,0:T(8,128)(2,1)} %pos_embed.1, f32[1,1024]{1,0:T(1,128)} %bitcast.7, f32[1,1024]{1,0:T(1,128)} %bitcast.8, ...), custom_call_target="tpu_custom_call" | custom-call | tf_op jit(solution)/shard_map/pallas_call | solution.py:489
  132.4 3.2 %copy.22 = bf16[32,32,1024]{2,1,0:T(8,128)(2,1)} copy(bf16[32,32,1024]{2,1,0:T(8,128)(2,1)} %shard_map.190) | data formatting | bytes 4194304
